TPU v7x, 32 devices: a whole 2x2x4 slice. The times are simulated.
32 devices in a mesh: dp: 2 (over y), ctx: 4 (over x, core), tensor: 4 (over z).
Axes of the slice: x: 2, y: 2, z: 4, core: 2. Of those that a mesh axis runs over, the one named last changes fastest.
Arguments:
- residual: bfloat16 [2048, 3584], P(('dp', 'ctx', 'tensor')), parts along dimension 0, may hold values from -6 to 6
- queries: bfloat16 [2048, 1024], P(('dp', 'ctx'), 'tensor'), parts along dimension 0, may hold values from -8 to 8
- key_heads: bfloat16 [2048, 512], P(('dp', 'ctx'), 'tensor'), parts along dimension 0, may hold values from -8 to 8
- value_heads: bfloat16 [2048, 512], P(('dp', 'ctx'), 'tensor'), parts along dimension 0, may hold values from -6 to 6
- doc_blocks: int32 [12], P('dp'), parts along dimension 0, may hold values from 1 to 16, 32 in all
- out_weight: bfloat16 [1024, 3584], P('tensor'), may hold values from -0.53125 to 0.53125
- post_gain: float32 [3584], replicated, may hold values from 0.1 to 1.9
- ffn_gain: float32 [3584], replicated, may hold values from 0.1 to 1.9
- gate_weight: bfloat16 [3584, 3584], P('ctx', 'tensor'), may hold values from -0.09375 to 0.09375
- up_weight: bfloat16 [3584, 3584], P('ctx', 'tensor'), may hold values from -0.09375 to 0.09375
Outputs:
- mixed_stream: bfloat16 [2048, 3584], P(('dp', 'ctx', 'tensor')), parts along dimension 0
- ffn_hidden: bfloat16 [2048, 3584], P(('dp', 'ctx'), 'tensor'), parts along dimension 0
There are 2 independent parts, one for each index of `dp`. A program takes and returns all parts, laid end to end along the dimension named above; an argument that names none is the same for every part. Nothing has to cross between parts.
Inputs may be any that keep to these rules, and one draw needn't show every extreme that they name: `doc_blocks`: the lengths, in blocks of 32 positions, of the 6 documents packed in order into the sequence; they sum to 32, and the longest has exactly 16 blocks.
All inputs are finite; a program needn't handle non-finite values.
Results may differ from a plain program's by a relative error of at most 0.025.
Values may be sent and summed in bfloat16 or wider, within the bound.
A program may use at most 64 MiB of HBM per device.

v0:
```python
import jax
import jax.numpy as jnp
from jax import lax
from jax.sharding import PartitionSpec as P

BLOCK = 32


SOFT_CAP = 50.0
NORM_EPS = 1e-06
ROPE_BASE = 10000.0


def partner_2(value, axis, apart):
    mask = 2**apart
    pairs = [(source, source ^ mask) for source in range(lax.axis_size(axis))]
    return lax.ppermute(value, axis, pairs)


def rope_angles(positions, head_size):
    halfway = head_size // 2
    frequency = ROPE_BASE ** (-(jnp.arange(halfway, dtype=jnp.float32) * 2.0) / head_size)
    angles = positions.astype(jnp.float32)[:, None] * frequency[None, :]
    return (jnp.cos(angles), jnp.sin(angles))


def rotate(heads_in, cosine, sine_value, head_size):
    rows_here = heads_in.shape[0]
    reshaped = heads_in.astype(jnp.float32).reshape(rows_here, -1, head_size)
    leading = reshaped[:, :, : head_size // 2]
    trailing = reshaped[:, :, head_size // 2 :]
    cos_wide = cosine[:, None, :]
    sin_wide = sine_value[:, None, :]
    turned = jnp.concatenate(
        [leading * cos_wide - trailing * sin_wide, trailing * cos_wide + leading * sin_wide], axis=2
    )
    return turned.reshape(rows_here, -1).astype(jnp.bfloat16)


def doc_of(positions, doc_blocks):
    doc_ends = jnp.cumsum(doc_blocks)
    passed = positions[:, None] // BLOCK >= doc_ends[None, :]
    return jnp.sum(passed.astype(jnp.int32), axis=1)


def rms_scale(values):
    return values * lax.rsqrt(jnp.mean(values * values, axis=-1, keepdims=True) + NORM_EPS)


def gelu_gate(gate_sum, up_sum):
    return (jax.nn.gelu(gate_sum, approximate=True) * up_sum).astype(jnp.bfloat16)


def attend(query_rows, query_pos, query_doc, key_rows, value_rows, key_pos, key_doc, score_scale):
    scores = (
        lax.dot_general(
            query_rows, key_rows, (((1,), (1,)), ((), ())), preferred_element_type=jnp.float32
        )
        * score_scale
    )
    capped = SOFT_CAP * jnp.tanh(scores / SOFT_CAP)
    visible = (key_pos[None, :] <= query_pos[:, None]) & (key_doc[None, :] == query_doc[:, None])
    weights = jnp.where(visible, jnp.exp(capped), 0.0).astype(jnp.bfloat16)
    numerator = jnp.dot(weights, value_rows, preferred_element_type=jnp.float32)
    denominator = jnp.sum(weights.astype(jnp.float32), axis=1)
    return (numerator, denominator)


def join_halves(own_part, other_part, own_first):
    return jnp.where(
        own_first,
        jnp.concatenate([own_part, other_part], axis=2),
        jnp.concatenate([other_part, own_part], axis=2),
    )


def per_device(
    residual,
    queries,
    key_heads,
    value_heads,
    doc_blocks,
    out_weight,
    post_gain,
    ffn_gain,
    gate_weight,
    up_weight,
):
    tok_rows = queries.shape[0]
    head_size = queries.shape[1]
    score_scale = head_size ** (-0.5)
    query_pos = lax.axis_index("ctx") * tok_rows + jnp.arange(tok_rows, dtype=jnp.int32)
    query_doc = doc_of(query_pos, doc_blocks)
    cosine, sine_value = rope_angles(query_pos, head_size)
    query_rot = rotate(queries, cosine, sine_value, head_size)
    stacked = jnp.stack([key_heads, value_heads])
    own_first = lax.axis_index("tensor") % 2 == 0
    partner = partner_2(stacked, "tensor", 0)
    joined = join_halves(stacked, partner, own_first)
    key_rot = rotate(joined[0], cosine, sine_value, head_size)
    shard_pair = (
        lax.all_gather(key_rot, "ctx", axis=0, tiled=True),
        lax.all_gather(joined[1], "ctx", axis=0, tiled=True),
    )
    key_pos = jnp.arange(shard_pair[0].shape[0], dtype=jnp.int32)
    numerator, denominator = attend(
        query_rot,
        query_pos,
        query_doc,
        shard_pair[0],
        shard_pair[1],
        key_pos,
        doc_of(key_pos, doc_blocks),
        score_scale,
    )
    attended = (numerator / denominator[:, None]).astype(jnp.bfloat16)
    attn_rows = lax.psum_scatter(
        jnp.dot(attended, out_weight, preferred_element_type=jnp.float32).astype(jnp.bfloat16),
        "tensor",
        scatter_dimension=0,
        tiled=True,
    ).astype(jnp.float32)
    mixed_stream = (residual.astype(jnp.float32) + rms_scale(attn_rows) * post_gain).astype(
        jnp.bfloat16
    )
    ffn_input = (rms_scale(mixed_stream.astype(jnp.float32)) * ffn_gain).astype(jnp.bfloat16)
    gathered_rows = lax.all_gather(ffn_input, "tensor", axis=0, tiled=True)
    shard_pair = (
        lax.all_gather(gate_weight, "ctx", axis=0, tiled=True),
        lax.all_gather(up_weight, "ctx", axis=0, tiled=True),
    )
    gate_part = jnp.dot(gathered_rows, shard_pair[0], preferred_element_type=jnp.float32)
    up_part = jnp.dot(gathered_rows, shard_pair[1], preferred_element_type=jnp.float32)
    ffn_hidden = gelu_gate(gate_part, up_part)
    return (mixed_stream, ffn_hidden)


def solution(mesh):
    in_specs = (
        P(("dp", "ctx", "tensor"), None),
        P(("dp", "ctx"), "tensor"),
        P(("dp", "ctx"), "tensor"),
        P(("dp", "ctx"), "tensor"),
        P("dp"),
        P("tensor", None),
        P(),
        P(),
        P("ctx", "tensor"),
        P("ctx", "tensor"),
    )
    out_specs = (P(("dp", "ctx", "tensor"), None), P(("dp", "ctx"), "tensor"))
    return jax.shard_map(
        per_device, mesh=mesh, in_specs=in_specs, out_specs=out_specs, check_vma=False
    )
```

profile of v0, /device:TPU:0, one launch (start us, length us, event | category | flops | bytes accessed | tf_op | source)
XLA Modules:
  0.0 227.5 jit_solution(10332107046243191215)
XLA Ops:
  7.2 1.0 pad_maximum_fusion
  8.2 3.1 %collective-permute-start = (bf16[2,256,128]{2,1,0:T(8,128)(2,1)S(1)}, bf16[2,256,128]{2,1,0:T(8,128)(2,1)S(1)}, u32[]{:S(2)}, u32[]{:S(2)}) collective-permute-start(bf16[2,256,128]{2,1,0:T(8,128)(2,1)S(1)} %pad_maximum_fusion), channel_id=1, source_target_pairs={{0,1},{1,0},{2,3},{3,2},{4,5},{5,4},{6,7},{7,6},{8,9},{9,8},{10,11... | collective-permute-start | bytes 393224 | tf_op jit(solution)/shard_map/ppermute | solution.py:17
  11.4 0.9 bitcast_convert_fusion
  12.3 0.8 reduce-window.8
  13.1 0.1 convert_reduce_fusion.2
  13.2 0.1 convert_reduce_fusion.1
  13.3 1.5 collective-permute-done
  14.9 1.0 maximum_select_fusion
  15.9 0.6 fusion.34
  16.5 7.3 %all-gather = bf16[1024,1,256]{2,0,1:T(8,128)(2,1)S(1)} all-gather(bf16[256,1,256]{2,0,1:T(8,128)(2,1)S(1)} %pad_maximum_fusion.1), channel_id=2, replica_groups=mesh['dp'=2,'ctx'=4,'tensor'=4] {'ctx'}, dimensions={0}, use_global_device_ids=true | all-gather | bytes 655360 | tf_op jit(solution)/shard_map/all_gather | solution.py:102
  23.9 7.3 %all-gather.1 = bf16[1,1024,256]{2,1,0:T(8,128)(2,1)S(1)} all-gather(bf16[1,256,256]{2,1,0:T(8,128)(2,1)S(1)} %get-tuple-element.8), channel_id=3, replica_groups=mesh['dp'=2,'ctx'=4,'tensor'=4] {'ctx'}, dimensions={1}, use_global_device_ids=true | all-gather | bytes 655360 | tf_op jit(solution)/shard_map/all_gather | solution.py:103
  31.1 0.7 convert_reduce_fusion
  31.8 2.4 %convolution_convert_fusion = bf16[256,3584]{1,0:T(8,128)(2,1)} fusion(bf16[256,3584]{1,0:T(8,128)(2,1)S(1)} %copy-done, bf16[256,1024]{1,0:T(8,128)(2,1)S(1)} %get-tuple-element.13, bf16[1,1024,256]{2,1,0:T(8,128)(2,1)S(1)} %all-gather.1, f32[256]{0:T(256)S(1)} %get-tuple-element.12), kind=kOutput, calls=%fused_computation | convolution fusion | flops 605028352 | bytes 4719616 | tf_op jit(solution)/shard_map/dot_general | solution.py:118
  34.3 40.2 %reduce-scatter.2.cloned.1.call-done = bf16[64,3584]{1,0:T(8,128)(2,1)} async-done(((bf16[256,3584]{1,0:T(8,128)(2,1)}), bf16[64,3584]{1,0:T(8,128)(2,1)}) %reduce-scatter.2.cloned.1.call-update) | async-done | bytes 458768 | tf_op jit(solution)/shard_map/reduce_scatter | solution.py:117
  74.5 1.2 fusion.8
  75.7 1.4 fusion.12
  77.2 0.9 fusion.14
  78.2 0.7 all-gather.8.cloned.1.call-update
  78.9 0.5 all-gather.10.cloned.1.call-update
  79.5 39.2 %all-gather.6.cloned.1.call-done = bf16[256,3584]{1,0:T(8,128)(2,1)} async-done(((bf16[64,3584]{1,0:T(8,128)(2,1)}), bf16[256,3584]{1,0:T(8,128)(2,1)}) %all-gather.6.cloned.1.call-update) | async-done | bytes 1835024 | tf_op jit(solution)/shard_map/all_gather | solution.py:127
  118.7 47.5 %all-gather.8.cloned.1.call-done = bf16[3584,896]{1,0:T(8,128)(2,1)} async-done(((bf16[896,896]{1,0:T(8,128)(2,1)}), bf16[3584,896]{1,0:T(8,128)(2,1)}) %all-gather.8.cloned.1.call-update) | async-done | bytes 6422544 | tf_op jit(solution)/shard_map/all_gather | solution.py:129
  166.2 5.5 %fusion.52 = f32[256,896]{1,0:T(8,128)S(1)} fusion(bf16[256,3584]{1,0:T(8,128)(2,1)} %all-gather.6.cloned.1.call-done, bf16[3584,896]{1,0:T(8,128)(2,1)} %all-gather.8.cloned.1.call-done), kind=kOutput, calls=%fused_computation.83 | convolution fusion | flops 1644167168 | bytes 9175040 | tf_op jit(solution)/shard_map/dot_general | solution.py:132
  171.6 43.1 %all-gather.10.cloned.1.call-done = bf16[3584,896]{1,0:T(8,128)(2,1)} async-done(((bf16[896,896]{1,0:T(8,128)(2,1)}), bf16[3584,896]{1,0:T(8,128)(2,1)}) %all-gather.10.cloned.1.call-update) | async-done | bytes 6422544 | tf_op jit(solution)/shard_map/all_gather | solution.py:130
  214.7 6.3 %fusion.5 = bf16[256,896]{1,0:T(8,128)(2,1)} fusion(bf16[256,3584]{1,0:T(8,128)(2,1)} %all-gather.6.cloned.1.call-done, bf16[3584,896]{1,0:T(8,128)(2,1)} %all-gather.10.cloned.1.call-done, f32[256,896]{1,0:T(8,128)S(1)} %fusion.52), kind=kOutput, calls=%fused_computation.9 | convolution fusion | flops 1646460928 | bytes 9633792 | tf_op jit(solution)/shard_map/dot_general | solution.py:133
  (24 shorter events, 0.3 us)
Async XLA Ops:
  7.2 24.7 %copy-start = (bf16[256,3584]{1,0:T(8,128)(2,1)S(1)}, bf16[256,3584]{1,0:T(8,128)(2,1)}, u32[]{:S(2)}) copy-start(bf16[256,3584]{1,0:T(8,128)(2,1)} %param.15) | copy-start | bytes 5505028
  7.2 67.3 %reduce-scatter.2.cloned.1.call-start = ((), (), s32[]{:S(2)}) async-start(), calls=%async_computation.1 | async-start | bytes 2293760 | tf_op jit(solution)/shard_map/reduce_scatter | solution.py:117
  8.2 6.6 %collective-permute-start = (bf16[2,256,128]{2,1,0:T(8,128)(2,1)S(1)}, bf16[2,256,128]{2,1,0:T(8,128)(2,1)S(1)}, u32[]{:S(2)}, u32[]{:S(2)}) collective-permute-start(bf16[2,256,128]{2,1,0:T(8,128)(2,1)S(1)} %pad_maximum_fusion), channel_id=1, source_target_pairs={{0,1},{1,0},{2,3},{3,2},{4,5},{5,4},{6,7},{7,6},{8,9},{9,8},{10,11... | collective-permute-start | bytes 393224 | tf_op jit(solution)/shard_map/ppermute | solution.py:17
  34.2 41.5 %copy-start.2 = (bf16[64,3584]{1,0:T(8,128)(2,1)S(1)}, bf16[64,3584]{1,0:T(8,128)(2,1)}, u32[]{:S(2)}) copy-start(bf16[64,3584]{1,0:T(8,128)(2,1)} %param.10) | copy-start | bytes 1376260
  34.2 41.5 %copy-start.3 = (f32[3584]{0:T(1024)S(1)}, f32[3584]{0:T(1024)}, u32[]{:S(2)}) copy-start(f32[3584]{0:T(1024)} %param.16) | copy-start | bytes 43012
  34.2 43.0 %copy-start.4 = (f32[3584]{0:T(1024)S(1)}, f32[3584]{0:T(1024)}, u32[]{:S(2)}) copy-start(f32[3584]{0:T(1024)} %param.17) | copy-start | bytes 43012
  34.2 84.4 %all-gather.6.cloned.1.call-start = ((), (), s32[]{:S(2)}) async-start(), calls=%async_computation.2 | async-start | bytes 2293760 | tf_op jit(solution)/shard_map/all_gather | solution.py:127
  77.1 2.3 %copy-start.1 = (bf16[64,3584]{1,0:T(8,128)(2,1)}, bf16[64,3584]{1,0:T(8,128)(2,1)S(1)}, u32[]{:S(2)}) copy-start(bf16[64,3584]{1,0:T(8,128)(2,1)S(1)} %get-tuple-element.3) | copy-start | bytes 1376260
  78.1 88.0 %all-gather.8.cloned.1.call-start = ((), (), s32[]{:S(2)}) async-start(), calls=%async_computation.3 | async-start | bytes 8028160 | tf_op jit(solution)/shard_map/all_gather | solution.py:129
  78.9 135.9 %all-gather.10.cloned.1.call-start = ((), (), s32[]{:S(2)}) async-start(), calls=%async_computation.4 | async-start | bytes 8028160 | tf_op jit(solution)/shard_map/all_gather | solution.py:130
Sparse Core Ops, SparseCore 0:
  34.4 40.0 reduce-scatter.1
  78.3 40.3 all-gather.5
  120.2 45.9 all-gather.7
  167.6 47.0 all-gather.9
where the time goes:
time: 228 us
  waiting for transfers between devices  173 us (76%)
  matrix products  14.8 us (6%)
  blocking collectives  14.6 us (6%)
  between operations  13.9 us (6%)
  other arithmetic  8.2 us (4%)
  starting transfers between devices  3.28 us (1%)
    all_gather x1, waiting for transfers between devices, per_device(): lax.all_gather(gate_weight, 'ctx', axis=0, tiled=True)  47.5 us
    all_gather x1, waiting for transfers between devices, per_device(): lax.all_gather(up_weight, 'ctx', axis=0, tiled=True)  43.1 us
    reduce_scatter x1, waiting for transfers between devices, per_device(): lax.psum_scatter(jnp.dot(attended, out_weight, preferred_element_type=jnp...  40.2 us
    all_gather x1, waiting for transfers between devices, per_device(): gathered_rows = lax.all_gather(ffn_input, 'tensor', axis=0, tiled=True)  39.2 us
    all_gather x1, blocking collectives, per_device(): lax.all_gather(key_rot, 'ctx', axis=0, tiled=True)  7.34 us
    all_gather x1, blocking collectives, per_device(): lax.all_gather(joined[1], 'ctx', axis=0, tiled=True)  7.26 us
    dot_general x1, matrix products, per_device(): jnp.dot(gathered_rows, shard_pair[1], preferred_element_type=jnp.float32)  6.25 us
    dot_general x1, matrix products, per_device(): jnp.dot(gathered_rows, shard_pair[0], preferred_element_type=jnp.float32)  5.45 us
  transfers between devices with their start and end apart: 5, of which 5 were waited for; matrix products, arithmetic and copies ran while one was open for 3% of the time, Pallas kernels for 0%

commit v1 on v0

--- a/solution.py
+++ b/solution.py
@@ -72,6 +72,76 @@
         jnp.concatenate([own_part, other_part], axis=2),
         jnp.concatenate([other_part, own_part], axis=2),
     )
+
+
+def relay_fits():
+    return lax.axis_size("ctx") == 4 and lax.axis_size("dp") == 2
+
+
+def relay_weights(gate_weight, up_weight):
+    if not relay_fits():
+        return None
+    rows = gate_weight.shape[0]
+    cut = -(-rows // 256) * 128
+    first_part = lax.axis_index("dp") == 0
+    carried = jnp.where(first_part, gate_weight, up_weight)
+    far = [partner_2(carried[:cut], "ctx", 1), partner_2(carried[cut:], "ctx", 1)]
+    near = [partner_2(weight, "ctx", 0) for weight in (gate_weight, up_weight)]
+    return near, far
+
+
+def hold_far(attended, relayed):
+    if relayed is None:
+        return attended, None
+    near, far = relayed
+    attended, near, far = lax.optimization_barrier((attended, near, far))
+    swapped = [partner_2(piece, "dp", 0) for piece in far]
+    far_near = [partner_2(piece, "ctx", 0) for piece in far]
+    return attended, (near, far, swapped, far_near)
+
+
+def hold_swapped(attn_rows, relayed):
+    if relayed is None:
+        return attn_rows, None
+    near, far, swapped, far_near = relayed
+    attn_rows, swapped, far_near = lax.optimization_barrier((attn_rows, swapped, far_near))
+    swapped_near = [partner_2(piece, "ctx", 0) for piece in swapped]
+    return attn_rows, (near, (far, swapped), (far_near, swapped_near))
+
+
+def project(rows_in, gate_weight, up_weight, relayed):
+    if relayed is None:
+        return tuple(
+            jnp.dot(
+                rows_in,
+                lax.all_gather(weight, "ctx", axis=0, tiled=True),
+                preferred_element_type=jnp.float32,
+            )
+            for weight in (gate_weight, up_weight)
+        )
+    depth = gate_weight.shape[0]
+    here = lax.axis_index("ctx")
+
+    def term(owner, offset, weight):
+        columns = lax.dynamic_slice_in_dim(rows_in, owner * depth + offset, weight.shape[0], axis=1)
+        return jnp.dot(columns, weight, preferred_element_type=jnp.float32)
+
+    near, across, across_near = relayed
+    gate_sum = term(here, 0, gate_weight) + term(here ^ 1, 0, near[0])
+    up_sum = term(here, 0, up_weight) + term(here ^ 1, 0, near[1])
+    sums = []
+    for which in range(2):
+        total = 0.0
+        for owner, pieces in ((here ^ 2, across[which]), (here ^ 3, across_near[which])):
+            offset = 0
+            for piece in pieces:
+                total = total + term(owner, offset, piece)
+                offset += piece.shape[0]
+        sums.append(total)
+    first_part = lax.axis_index("dp") == 0
+    gate_sum = gate_sum + jnp.where(first_part, sums[0], sums[1])
+    up_sum = up_sum + jnp.where(first_part, sums[1], sums[0])
+    return gate_sum, up_sum
 
 
 def per_device(
@@ -86,6 +156,7 @@
     gate_weight,
     up_weight,
 ):
+    relayed = relay_weights(gate_weight, up_weight)
     tok_rows = queries.shape[0]
     head_size = queries.shape[1]
     score_scale = head_size ** (-0.5)
@@ -114,23 +185,20 @@
         score_scale,
     )
     attended = (numerator / denominator[:, None]).astype(jnp.bfloat16)
+    attended, relayed = hold_far(attended, relayed)
     attn_rows = lax.psum_scatter(
         jnp.dot(attended, out_weight, preferred_element_type=jnp.float32).astype(jnp.bfloat16),
         "tensor",
         scatter_dimension=0,
         tiled=True,
     ).astype(jnp.float32)
+    attn_rows, relayed = hold_swapped(attn_rows, relayed)
     mixed_stream = (residual.astype(jnp.float32) + rms_scale(attn_rows) * post_gain).astype(
         jnp.bfloat16
     )
     ffn_input = (rms_scale(mixed_stream.astype(jnp.float32)) * ffn_gain).astype(jnp.bfloat16)
     gathered_rows = lax.all_gather(ffn_input, "tensor", axis=0, tiled=True)
-    shard_pair = (
-        lax.all_gather(gate_weight, "ctx", axis=0, tiled=True),
-        lax.all_gather(up_weight, "ctx", axis=0, tiled=True),
-    )
-    gate_part = jnp.dot(gathered_rows, shard_pair[0], preferred_element_type=jnp.float32)
-    up_part = jnp.dot(gathered_rows, shard_pair[1], preferred_element_type=jnp.float32)
+    gate_part, up_part = project(gathered_rows, gate_weight, up_weight, relayed)
     ffn_hidden = gelu_gate(gate_part, up_part)
     return (mixed_stream, ffn_hidden)
 

time: 228 us -> 177 us (0.78)
  waiting for transfers between devices: 173 us -> 77.5 us
  blocking collectives: 14.6 us -> 40.4 us
  starting transfers between devices: 3.28 us -> 8.56 us
  matrix products: 14.8 us -> 20 us
  local copies, waits for them, and re-layouts: 0.03 us -> 3.6 us
  other arithmetic: 8.2 us -> 11.5 us
    all_gather x2 -> x0, waiting for transfers between devices: 90.6 us -> none  [the longest x1 47.5 us: per_device(): lax.all_gather(gate_weight, 'ctx', axis=0, tiled=True)]
    all_gather x1, blocking collectives: 7.34 us -> 33.2 us  [per_device(): lax.all_gather(key_rot, 'ctx', axis=0, tiled=True)]
    dot_general x2 -> x13, matrix products: 11.7 us -> 17.4 us  [the longest x12 17.1 us: term(): return jnp.dot(columns, weight, preferred_element_type=jnp.float32)]
    ppermute x1 -> x11, starting transfers between devices: 3.12 us -> 8.48 us  [partner_2(): return lax.ppermute(value, axis, pairs)]
    reduce_scatter x1, waiting for transfers between devices: 40.2 us -> 37.5 us  [per_device(): lax.psum_scatter(jnp.dot(attended, out_weight, preferred_element_type=jnp...]
  transfers between devices with their start and end apart: 5 -> 13, of which waited for: 5 -> 2; matrix products, arithmetic and copies ran while one was open for 3% -> 11% of each run, Pallas kernels for 0% -> 0%
where the time goes in v1:
time: 177 us; the launch traced here: 176 us
  waiting for transfers between devices  77.5 us (44%)
  blocking collectives  40.4 us (23%)
  matrix products  20 us (11%)
  between operations  14.5 us (8%)
  other arithmetic  11.5 us (6%)
  starting transfers between devices  8.56 us (5%)
  local copies, waits for them, and re-layouts  3.6 us (2%)
    all_gather x1, waiting for transfers between devices, per_device(): gathered_rows = lax.all_gather(ffn_input, 'tensor', axis=0, tiled=True)  39.9 us
    reduce_scatter x1, waiting for transfers between devices, per_device(): lax.psum_scatter(jnp.dot(attended, out_weight, preferred_element_type=jnp...  37.5 us
    all_gather x1, blocking collectives, per_device(): lax.all_gather(key_rot, 'ctx', axis=0, tiled=True)  33.2 us
    dot_general x12, matrix products, term(): return jnp.dot(columns, weight, preferred_element_type=jnp.float32)  17.1 us
    ppermute x11, starting transfers between devices, partner_2(): return lax.ppermute(value, axis, pairs)  8.48 us
    all_gather x1, blocking collectives, per_device(): lax.all_gather(joined[1], 'ctx', axis=0, tiled=True)  7.26 us
  transfers between devices with their start and end apart: 13, of which 2 were waited for; matrix products, arithmetic and copies ran while one was open for 11% of the time, Pallas kernels for 0%

profile of v1, /device:TPU:0, one launch (start us, length us, event | category | flops | bytes accessed | tf_op | source)
XLA Modules:
  0.0 176.1 jit_solution(14855796329275414830)
XLA Ops:
  7.2 1.7 pad_maximum_fusion
  8.9 3.1 %collective-permute-start = (bf16[2,256,128]{2,1,0:T(8,128)(2,1)}, bf16[2,256,128]{2,1,0:T(8,128)(2,1)}, u32[]{:S(2)}, u32[]{:S(2)}) collective-permute-start(bf16[2,256,128]{2,1,0:T(8,128)(2,1)} %pad_maximum_fusion), channel_id=1, source_target_pairs={{0,1},{1,0},{2,3},{3,2},{4,5},{5,4},{6,7},{7,6},{8,9},{9,8},{10,11... | collective-permute-start | bytes 393224 | tf_op jit(solution)/shard_map/ppermute | solution.py:17
  12.5 1.6 broadcast_select_fusion
  14.1 1.0 slice.38
  15.1 1.5 collective-permute-start.3
  18.0 1.6 bitcast_convert_fusion
  20.1 1.1 maximum_select_fusion
  21.2 1.6 fusion.56
  22.8 33.2 %all-gather = bf16[1024,1,256]{2,0,1:T(8,128)(2,1)S(1)} all-gather(bf16[256,1,256]{2,0,1:T(8,128)(2,1)S(1)} %pad_maximum_fusion.1), channel_id=2, replica_groups=mesh['dp'=2,'ctx'=4,'tensor'=4] {'ctx'}, dimensions={0}, use_global_device_ids=true | all-gather | bytes 655360 | tf_op jit(solution)/shard_map/all_gather | solution.py:173
  56.0 7.3 %all-gather.1 = bf16[1,1024,256]{2,1,0:T(8,128)(2,1)S(1)} all-gather(bf16[1,256,256]{2,1,0:T(8,128)(2,1)S(1)} %get-tuple-element.28), channel_id=3, replica_groups=mesh['dp'=2,'ctx'=4,'tensor'=4] {'ctx'}, dimensions={1}, use_global_device_ids=true | all-gather | bytes 655360 | tf_op jit(solution)/shard_map/all_gather | solution.py:174
  64.3 1.9 %convolution_convert_fusion = bf16[256,3584]{1,0:T(8,128)(2,1)} fusion(bf16[256,256]{1,0:T(8,128)(2,1)S(1)} %fusion.13, bf16[256,3584]{1,0:T(8,128)(2,1)S(1)} %copy-done), kind=kOutput, calls=%fused_computation | convolution fusion | flops 470679552 | bytes 3801088 | tf_op jit(solution)/shard_map/dot_general | solution.py:190
  66.3 1.6 collective-permute-start.5
  68.6 37.5 %reduce-scatter.2.cloned.1.call-done = bf16[64,3584]{1,0:T(8,128)(2,1)} async-done(((bf16[256,3584]{1,0:T(8,128)(2,1)}), bf16[64,3584]{1,0:T(8,128)(2,1)}) %reduce-scatter.2.cloned.1.call-update) | async-done | bytes 458768 | tf_op jit(solution)/shard_map/reduce_scatter | solution.py:189
  106.1 1.1 convert_element_type.77
  107.4 1.4 fusion.15
  110.4 39.9 %all-gather.4.cloned.1.call-done = bf16[256,3584]{1,0:T(8,128)(2,1)} async-done(((bf16[64,3584]{1,0:T(8,128)(2,1)}), bf16[256,3584]{1,0:T(8,128)(2,1)}) %all-gather.4.cloned.1.call-update) | async-done | bytes 1835024 | tf_op jit(solution)/shard_map/all_gather | solution.py:200
  150.3 1.7 fusion.53
  152.1 1.6 fusion.51
  153.7 1.5 fusion.49
  155.3 1.6 fusion.47
  156.9 1.6 fusion.35
  160.7 1.6 fusion.33
  162.3 1.7 fusion.9
  166.3 3.0 %fusion.12 = bf16[256,896]{1,0:T(8,128)(2,1)} fusion(f32[256,896]{1,0:T(8,128)S(1)} %fusion.24, f32[256,896]{1,0:T(8,128)S(1)} %fusion.29, bf16[896,896]{1,0:T(8,128)(2,1)} %collective-permute-done.2, f32[256,896]{1,0:T(8,128)S(1)} %fusion.7, f32[256,896]{1,0:T(8,128)S(1)} %fusion.9, pred[]{:T(512)S(6)} %eq.26, bf16[256,3584]{1,0:T(8,128)(2,1)S(1)} %copy-done.1, ...), kind=kOutput, calls=%fused_computation.20 | convolution fusion | flops 412188672 | bytes 6193157 | tf_op jit(solution)/shard_map/dot_general | solution.py:127
  (65 shorter events, 10.3 us)
Async XLA Ops:
  7.2 57.1 %copy-start = (bf16[256,3584]{1,0:T(8,128)(2,1)S(1)}, bf16[256,3584]{1,0:T(8,128)(2,1)}, u32[]{:S(2)}) copy-start(bf16[256,3584]{1,0:T(8,128)(2,1)} %param.15) | copy-start | bytes 5505028
  7.2 99.0 %reduce-scatter.2.cloned.1.call-start = ((), (), s32[]{:S(2)}) async-start(), calls=%async_computation.1 | async-start | bytes 2293760 | tf_op jit(solution)/shard_map/reduce_scatter | solution.py:189
  8.9 11.2 %collective-permute-start = (bf16[2,256,128]{2,1,0:T(8,128)(2,1)}, bf16[2,256,128]{2,1,0:T(8,128)(2,1)}, u32[]{:S(2)}, u32[]{:S(2)}) collective-permute-start(bf16[2,256,128]{2,1,0:T(8,128)(2,1)} %pad_maximum_fusion), channel_id=1, source_target_pairs={{0,1},{1,0},{2,3},{3,2},{4,5},{5,4},{6,7},{7,6},{8,9},{9,8},{10,11... | collective-permute-start | bytes 393224 | tf_op jit(solution)/shard_map/ppermute | solution.py:17
  11.9 52.3 %collective-permute-start.1 = (bf16[896,896]{1,0:T(8,128)(2,1)}, bf16[896,896]{1,0:T(8,128)(2,1)S(1)}, u32[]{:S(2)}, u32[]{:S(2)}) collective-permute-start(bf16[896,896]{1,0:T(8,128)(2,1)} %param.18), channel_id=1, source_target_pairs={{0,4},{4,0},{8,12},{12,8},{1,5},{5,1},{9,13},{13,9},{2,6},{6,2},{1... | collective-permute-start | bytes 4816904 | tf_op jit(solution)/shard_map/ppermute | solution.py:17
  11.9 52.3 %collective-permute-start.2 = (bf16[896,896]{1,0:T(8,128)(2,1)}, bf16[896,896]{1,0:T(8,128)(2,1)}, u32[]{:S(2)}, u32[]{:S(2)}) collective-permute-start(bf16[896,896]{1,0:T(8,128)(2,1)} %param.19), channel_id=1, source_target_pairs={{0,4},{4,0},{8,12},{12,8},{1,5},{5,1},{9,13},{13,9},{2,6},{6,2},{1... | collective-permute-start | bytes 4816904 | tf_op jit(solution)/shard_map/ppermute | solution.py:17
  14.1 5.6 %copy-start.10 = (s32[6]{0:T(128)S(1)}, s32[6]{0:T(128)}, u32[]{:S(2)}) copy-start(s32[6]{0:T(128)} %param.14) | copy-start | bytes 76
  14.1 6.0 %copy-start.7 = (bf16[256,128]{1,0:T(8,128)(2,1)S(1)}, bf16[256,128]{1,0:T(8,128)(2,1)}, u32[]{:S(2)}) copy-start(bf16[256,128]{1,0:T(8,128)(2,1)} %param.13) | copy-start | bytes 196612
  15.1 49.2 %collective-permute-start.3 = (bf16[512,896]{1,0:T(8,128)(2,1)}, bf16[512,896]{1,0:T(8,128)(2,1)}, u32[]{:S(2)}, u32[]{:S(2)}) collective-permute-start(bf16[512,896]{1,0:T(8,128)(2,1)} %slice.38), channel_id=1, source_target_pairs={{0,8},{4,12},{8,0},{12,4},{1,9},{5,13},{9,1},{13,5},{2,10},{6,14},... | collective-permute-start | bytes 2752520 | tf_op jit(solution)/shard_map/ppermute | solution.py:17
  17.5 46.7 %collective-permute-start.4 = (bf16[384,896]{1,0:T(8,128)(2,1)}, bf16[384,896]{1,0:T(8,128)(2,1)}, u32[]{:S(2)}, u32[]{:S(2)}) collective-permute-start(bf16[384,896]{1,0:T(8,128)(2,1)} %slice.39), channel_id=1, source_target_pairs={{0,8},{4,12},{8,0},{12,4},{1,9},{5,13},{9,1},{13,5},{2,10},{6,14},... | collective-permute-start | bytes 2064392 | tf_op jit(solution)/shard_map/ppermute | solution.py:17
  64.3 1.9 %copy-start.5 = (bf16[896,896]{1,0:T(8,128)(2,1)}, bf16[896,896]{1,0:T(8,128)(2,1)S(1)}, u32[]{:S(2)}) copy-start(bf16[896,896]{1,0:T(8,128)(2,1)S(1)} %collective-permute-done.1) | copy-start | bytes 4816900
  66.2 41.2 %copy-start.8 = (f32[3584]{0:T(1024)S(1)}, f32[3584]{0:T(1024)}, u32[]{:S(2)}) copy-start(f32[3584]{0:T(1024)} %param.16) | copy-start | bytes 43012
  66.2 42.6 %copy-start.9 = (f32[3584]{0:T(1024)S(1)}, f32[3584]{0:T(1024)}, u32[]{:S(2)}) copy-start(f32[3584]{0:T(1024)} %param.17) | copy-start | bytes 43012
  66.2 84.1 %all-gather.4.cloned.1.call-start = ((), (), s32[]{:S(2)}) async-start(), calls=%async_computation.2 | async-start | bytes 2293760 | tf_op jit(solution)/shard_map/all_gather | solution.py:200
  66.3 41.0 %collective-permute-start.5 = (bf16[512,896]{1,0:T(8,128)(2,1)}, bf16[512,896]{1,0:T(8,128)(2,1)S(1)}, u32[]{:S(2)}, u32[]{:S(2)}) collective-permute-start(bf16[512,896]{1,0:T(8,128)(2,1)} %collective-permute-done.3), channel_id=1, source_target_pairs={{0,16},{16,0},{1,17},{17,1},{2,18},{18,2},{3,19},{19,3},{4,20},{20... | collective-permute-start | bytes 2752520 | tf_op jit(solution)/shard_map/ppermute | solution.py:17
  67.9 39.4 %collective-permute-start.7 = (bf16[512,896]{1,0:T(8,128)(2,1)}, bf16[512,896]{1,0:T(8,128)(2,1)}, u32[]{:S(2)}, u32[]{:S(2)}) collective-permute-start(bf16[512,896]{1,0:T(8,128)(2,1)} %collective-permute-done.3), channel_id=1, source_target_pairs={{0,4},{4,0},{8,12},{12,8},{1,5},{5,1},{9,13},{13,9},{2,6},{6,2},{1... | collective-permute-start | bytes 2752520 | tf_op jit(solution)/shard_map/ppermute | solution.py:17
  67.9 39.3 %collective-permute-start.6 = (bf16[384,896]{1,0:T(8,128)(2,1)}, bf16[384,896]{1,0:T(8,128)(2,1)}, u32[]{:S(2)}, u32[]{:S(2)}) collective-permute-start(bf16[384,896]{1,0:T(8,128)(2,1)} %collective-permute-done.4), channel_id=1, source_target_pairs={{0,16},{16,0},{1,17},{17,1},{2,18},{18,2},{3,19},{19,3},{4,20},{20... | collective-permute-start | bytes 2064392 | tf_op jit(solution)/shard_map/ppermute | solution.py:17
  68.4 38.8 %collective-permute-start.8 = (bf16[384,896]{1,0:T(8,128)(2,1)}, bf16[384,896]{1,0:T(8,128)(2,1)}, u32[]{:S(2)}, u32[]{:S(2)}) collective-permute-start(bf16[384,896]{1,0:T(8,128)(2,1)} %collective-permute-done.4), channel_id=1, source_target_pairs={{0,4},{4,0},{8,12},{12,8},{1,5},{5,1},{9,13},{13,9},{2,6},{6,2},{1... | collective-permute-start | bytes 2064392 | tf_op jit(solution)/shard_map/ppermute | solution.py:17
  108.8 44.9 %copy-start.4 = (bf16[64,3584]{1,0:T(8,128)(2,1)}, bf16[64,3584]{1,0:T(8,128)(2,1)S(1)}, u32[]{:S(2)}) copy-start(bf16[64,3584]{1,0:T(8,128)(2,1)S(1)} %get-tuple-element.23) | copy-start | bytes 1376260
  109.9 45.4 %collective-permute-start.10 = (bf16[384,896]{1,0:T(8,128)(2,1)}, bf16[384,896]{1,0:T(8,128)(2,1)}, u32[]{:S(2)}, u32[]{:S(2)}) collective-permute-start(bf16[384,896]{1,0:T(8,128)(2,1)} %collective-permute-done.6), channel_id=1, source_target_pairs={{0,4},{4,0},{8,12},{12,8},{1,5},{5,1},{9,13},{13,9},{2,6},{6,2},{1... | collective-permute-start | bytes 2064392 | tf_op jit(solution)/shard_map/ppermute | solution.py:17
  109.9 50.7 %collective-permute-start.9 = (bf16[512,896]{1,0:T(8,128)(2,1)S(1)}, bf16[512,896]{1,0:T(8,128)(2,1)}, u32[]{:S(2)}, u32[]{:S(2)}) collective-permute-start(bf16[512,896]{1,0:T(8,128)(2,1)S(1)} %collective-permute-done.5), channel_id=1, source_target_pairs={{0,4},{4,0},{8,12},{12,8},{1,5},{5,1},{9,13},{13,9},{2,6},{6,2},{1... | collective-permute-start | bytes 2752520 | tf_op jit(solution)/shard_map/ppermute | solution.py:17
  150.3 3.4 %copy-start.1 = (bf16[256,3584]{1,0:T(8,128)(2,1)S(1)}, bf16[256,3584]{1,0:T(8,128)(2,1)}, u32[]{:S(2)}) copy-start(bf16[256,3584]{1,0:T(8,128)(2,1)} %all-gather.4.cloned.1.call-done) | copy-start | bytes 5505028
  155.3 3.3 %copy-start.2 = (bf16[896,896]{1,0:T(8,128)(2,1)S(1)}, bf16[896,896]{1,0:T(8,128)(2,1)}, u32[]{:S(2)}) copy-start(bf16[896,896]{1,0:T(8,128)(2,1)} %param.18) | copy-start | bytes 4816900
  158.6 1.4 copy-start.3
  164.0 1.4 copy-start.6
Sparse Core Ops, SparseCore 0:
  66.3 39.7 reduce-scatter.1
  109.9 40.3 all-gather.3
